TPU v7x, 32 devices: a whole 2x2x4 slice. The times are simulated.
32 devices in a mesh: src: 8 (over y, x, core), tgt: 4 (over z).
Axes of the slice: x: 2, y: 2, z: 4, core: 2. Of those that a mesh axis runs over, the one named last changes fastest.
Arguments:
- src_points: bfloat16 [64, 4096], P(None, ('src', 'tgt')), may hold values from -3 to 3
- tgt_points: bfloat16 [64, 1024], P(None, 'tgt'), may hold values from -3 to 3
- src_log_mass: float32 [4096], P(('src', 'tgt')), may hold values from -4 to 4
- tgt_log_mass: bfloat16 [1024], P('tgt'), may hold values from -4 to 4
- tgt_potential: bfloat16 [1024], P('tgt'), may hold values from -18 to 168
- src_cluster: int32 [4096], P(('src', 'tgt')), may hold values from 0 to 63, as said below
- tgt_cluster: int32 [1024], P('tgt'), may hold values from 0 to 63, as said below
- kept_pairs: int32 [1024, 2], replicated, may hold values from 0 to 63, as said below
Outputs:
- new_src_potential: float32 [4096], P(('src', 'tgt'))
- new_tgt_potential: float32 [1024], P('tgt')
Inputs may be any that keep to these rules, and one draw needn't show every extreme that they name: `src_cluster`: never falls along the cells; every cluster holds at least one cell. `tgt_cluster`: never falls along the cells; every cluster holds at least one cell. `kept_pairs`: each pair stands once; every cluster of either day is in some pair.
All inputs are finite; a program needn't handle non-finite values.
Results may differ from a plain program's by a relative error of at most 0.00045.
Values may be sent and summed in bfloat16 or wider, within the bound.
No kernel may reach another device: no remote copies, remote signals or barrier semaphores. Data moves between devices by JAX's collectives and lax.ppermute only.
A program may use at most 128 MiB of HBM per device.

v0:
```python
import math

import jax
import jax.numpy as jnp
from jax import lax
from jax.sharding import PartitionSpec as P

DIM = 64
CLUSTERS = 64


FLOOR_VALUE = -1e30
EPSILON = 1.0
MASS_FACTOR = 10.0 / 11.0
TILE_WIDTH = 2048


def square_norms(points):
    widened = points.astype(jnp.float32)
    return jnp.sum(widened * widened, axis=0)


def cross_products(left_rows, right_rows):
    return lax.dot_general(
        left_rows, right_rows, (((0,), (0,)), ((), ())), preferred_element_type=jnp.float32
    )


def build_grid(kept_pairs, labels):
    src_side = (kept_pairs[:, 0][:, None] == labels[None, :]).astype(jnp.float32)
    tgt_side = (kept_pairs[:, 1][:, None] == labels[None, :]).astype(jnp.float32)
    return jnp.dot(src_side.T, tgt_side, preferred_element_type=jnp.float32)


def body(
    src_points,
    tgt_points,
    src_log_mass,
    tgt_log_mass,
    tgt_potential,
    src_cluster,
    tgt_cluster,
    kept_pairs,
):
    labels = jnp.arange(CLUSTERS, dtype=jnp.int32)
    pair_grid = build_grid(kept_pairs, labels)
    src_norms = square_norms(src_points)
    src_onehot = (src_cluster[:, None] == labels[None, :]).astype(jnp.float32)
    row_grid = jnp.dot(src_onehot, pair_grid, preferred_element_type=jnp.float32)
    reach = jnp.max(row_grid, axis=0)
    row_table = row_grid.astype(jnp.bfloat16)
    row_count = src_points.shape[1]
    block_width = tgt_points.shape[1]
    side_terms = jnp.stack([tgt_potential, tgt_log_mass, tgt_cluster.astype(jnp.bfloat16)], axis=0)
    packed = jnp.concatenate([tgt_points, side_terms], axis=0)

    def unpack(tile):
        tile_points = tile[:DIM]
        tile_labels = tile[DIM + 2].astype(jnp.int32)
        tgt_onehot = labels[:, None] == tile_labels[None, :]
        has_work = jnp.sum(reach * jnp.max(tgt_onehot.astype(jnp.float32), axis=1)) > 0.5
        return (tile_points, tgt_onehot.astype(jnp.bfloat16), has_work)

    def row_tile(running, tile):
        tile_points, tgt_onehot, has_work = unpack(tile)

        def row_compute(current):
            peak_row, sum_row = current
            kept_mask = jnp.dot(row_table, tgt_onehot, preferred_element_type=jnp.float32) > 0.5
            tile_bias = (
                tile[DIM].astype(jnp.float32) - square_norms(tile_points)
            ) / EPSILON + tile[DIM + 1].astype(jnp.float32)
            scores = (
                tile_bias[None, :]
                - (src_norms[:, None] - 2.0 * cross_products(src_points, tile_points)) / EPSILON
            )
            scores = jnp.where(kept_mask, scores, FLOOR_VALUE)
            new_peak = jnp.maximum(peak_row, jnp.max(scores, axis=1))
            weights = jnp.where(kept_mask, jnp.exp(scores - new_peak[:, None]), 0.0)
            return (new_peak, sum_row * jnp.exp(peak_row - new_peak) + jnp.sum(weights, axis=1))

        return lax.cond(has_work, row_compute, lambda current: current, running)

    start_state = (
        jnp.full((row_count,), FLOOR_VALUE, jnp.float32),
        jnp.zeros((row_count,), jnp.float32),
    )
    targets = lax.all_gather(packed, "tgt", axis=1, tiled=True)
    columns = targets.shape[1]
    tile_width = math.gcd(columns, TILE_WIDTH)

    def advance(number, current):
        return row_tile(
            current, lax.dynamic_slice_in_dim(targets, number * tile_width, tile_width, 1)
        )

    peak_row, sum_row = lax.fori_loop(0, columns // tile_width, advance, start_state)
    new_src = -MASS_FACTOR * EPSILON * (peak_row + jnp.log(sum_row))
    col_bias = (new_src - src_norms) / EPSILON + src_log_mass
    column_targets = lax.all_gather(packed, "tgt", axis=1, tiled=True)
    columns = column_targets.shape[1]
    column_tile_width = math.gcd(columns, TILE_WIDTH)

    def column_tile(number):
        tile = lax.dynamic_slice_in_dim(
            column_targets, number * column_tile_width, column_tile_width, 1
        )
        tile_points, tgt_onehot, has_work = unpack(tile)

        def column_compute(unused):
            kept_mask = jnp.dot(row_table, tgt_onehot, preferred_element_type=jnp.float32) > 0.5
            scores = (
                col_bias[:, None]
                - (
                    square_norms(tile_points)[None, :]
                    - 2.0 * cross_products(src_points, tile_points)
                )
                / EPSILON
            )
            scores = jnp.where(kept_mask, scores, FLOOR_VALUE)
            highest = jnp.max(scores, axis=0)
            weights = jnp.where(kept_mask, jnp.exp(scores - highest[None, :]), 0.0)
            return (highest, jnp.sum(weights, axis=0))

        def skipped(unused):
            return (
                jnp.full((column_tile_width,), FLOOR_VALUE, jnp.float32),
                jnp.zeros((column_tile_width,), jnp.float32),
            )

        return lax.cond(has_work, column_compute, skipped, 0)

    peaks, totals = lax.map(column_tile, jnp.arange(columns // column_tile_width, dtype=jnp.int32))
    piece_peak = peaks.reshape(columns)
    piece_sum = totals.reshape(columns)
    stacked = jnp.stack([piece_peak, piece_sum], axis=0)
    col_peak, col_sum = (stacked[0], stacked[1])
    block_offset = lax.axis_index("tgt") * block_width
    global_peak = lax.pmax(col_peak, ("src", "tgt"))
    rescaled = col_sum * jnp.exp(col_peak - global_peak)
    own_share = lax.psum_scatter(rescaled, "tgt", scatter_dimension=0, tiled=True)
    own_sum = lax.psum(own_share, "src")
    own_peak = lax.dynamic_slice_in_dim(global_peak, block_offset, block_width, 0)
    new_tgt = -MASS_FACTOR * EPSILON * (own_peak + jnp.log(own_sum))
    return (new_src, new_tgt)


def solution(mesh):
    in_specs = (
        P(None, ("src", "tgt")),
        P(None, "tgt"),
        P(("src", "tgt")),
        P("tgt"),
        P("tgt"),
        P(("src", "tgt")),
        P("tgt"),
        P(),
    )
    out_specs = (P(("src", "tgt")), P("tgt"))
    return jax.shard_map(body, mesh=mesh, in_specs=in_specs, out_specs=out_specs, check_vma=False)
```

profile of v0, /device:TPU:0, one launch (start us, length us, event | category | flops | bytes accessed | tf_op | source)
XLA Modules:
  0.0 92.5 jit_solution(2774065129864218746)
XLA Ops:
  0.6 0.7 convert_element_type.50
  1.3 0.6 copy-done.4
  2.0 0.6 copy-done.5
  2.6 0.8 pad_maximum_fusion
  3.4 15.2 %all_gather.4 = bf16[67,1024]{1,0:T(8,128)(2,1)S(1)} all-gather(bf16[67,256]{1,0:T(8,128)(2,1)S(1)} %pad_maximum_fusion), channel_id=1, replica_groups=mesh['src'=8,'tgt'=4] {'tgt'}, dimensions={1}, use_global_device_ids=true | all-gather | bytes 171520 | tf_op jit(solution)/shard_map/all_gather | solution.py:88
  18.6 0.0 copy-start.1
  18.6 0.7 copy-done.1
  19.3 0.6 copy-done.6
  20.0 0.9 fusion.18
  20.8 0.0 copy-start
  20.9 0.7 copy-done
  21.6 0.1 convert_reduce_fusion
  21.7 0.6 multiply_reduce_fusion.3
  23.0 1.0 %conditional.2 = ((f32[128]{0:T(128)S(1)}, f32[128]{0:T(128)S(1)})) conditional(s32[]{:T(128)} %convert_element_type.52, (f32[128]{0:T(128)S(1)}, f32[128]{0:T(128)S(1)}) %tuple.37, (bf16[128,64]{0,1:T(8,128)(2,1)S(1)}, bf16[64,1024]{1,0:T(8,128)(2,1)S(1)}, bf16[67,1024]{1,0:T(8,128)(2,1)S(1)}, bf16[64,1024]{1,0:T(8,128)(2,1)S(1)}, f32[128]{0:T(128)S(1)}, ...), branch_computations={%region_4.5_spmd, %region_5.9_spmd} | conditional | flops 34934016 | bytes 1895448 | solution.py:82
  23.0 0.3 convolution_compare_fusion
  23.3 0.4 fusion.16
  23.7 0.3 select_reduce_fusion
  24.0 0.0 copy-start.3
  24.0 0.0 copy-start.2
  24.0 0.6 copy-done.2
  24.7 2.0 %conditional.3 = (f32[1024]{0:T(1024)}, f32[1024]{0:T(1024)S(1)}) conditional(s32[]{:T(128)} %convert_element_type.52, () %tuple.39, (bf16[128,64]{0,1:T(8,128)(2,1)S(1)}, bf16[64,1024]{1,0:T(8,128)(2,1)S(1)}, f32[128]{0:T(128)S(1)}, f32[128]{0:T(128)S(1)}, f32[128]{0:T(128)S(1)}, /*index=5*/bf16[64,1024]{1,0:T(8,128)(2,1)S(1)}, ...), branch_computations={%region_9.10_spmd, %region_10.14_spmd} | conditional | flops 34927872 | bytes 1890832 | solution.py:131
  24.7 0.2 convolution_compare_fusion.1
  25.0 0.9 fusion.17
  25.9 0.8 select_reduce_fusion.1
  26.7 40.9 %pmax.7 = f32[1024]{0:T(1024)S(1)} all-reduce(f32[1024]{0:T(1024)} %get-tuple-element.126), channel_id=1, replica_groups=mesh['src'=8,'tgt'=4] {'src','tgt'}, use_global_device_ids=true, to_apply=%region_14.15 | all-reduce | flops 1024 | bytes 8192 | tf_op jit(solution)/shard_map/pmax | solution.py:139
  67.6 0.7 exponential_multiply_fusion
  68.3 9.8 %all-reduce = f32[1024]{0:T(1024)S(1)} all-reduce(f32[1024]{0:T(1024)S(1)} %exponential_multiply_fusion), channel_id=2, replica_groups=mesh['src'=8,'tgt'=4] {'tgt'}, use_global_device_ids=true, to_apply=%region_15.16.clone | all-reduce | flops 1024 | bytes 8192
  78.1 0.7 copy-done.7
  78.8 0.6 dynamic-slice
  80.0 0.1 dynamic-slice.1
  80.1 11.8 %psum.7 = f32[256]{0:T(256)S(1)} all-reduce(f32[256]{0:T(256)S(1)} %dynamic-slice.1), channel_id=1, replica_groups=mesh['src'=8,'tgt'=4] {'src'}, use_global_device_ids=true, to_apply=%region_16.0 | all-reduce | flops 256 | bytes 2048 | tf_op jit(solution)/shard_map/psum | solution.py:142
  91.9 0.6 add_multiply_fusion
  (23 shorter events, 0.2 us)
Async XLA Ops:
  1.3 0.7 copy-start.4
  2.0 0.7 copy-start.5
  18.6 0.7 copy-start.1
  19.3 0.7 copy-start.6
  20.8 0.7 copy-start
  24.0 0.7 copy-start.3
  24.0 0.7 copy-start.2
  78.1 0.7 copy-start.7
where the time goes:
time: 93.2 us; the launch traced here: 92.5 us
  blocking collectives  77.7 us (83%)
  local copies, waits for them, and re-layouts  5.31 us (6%)
  other arithmetic  4.79 us (5%)
  matrix products  2.63 us (3%)
  between operations  2.03 us (2%)
    pmax x1, blocking collectives, body(): global_peak = lax.pmax(col_peak, ('src', 'tgt'))  40.9 us
    all_gather x1, blocking collectives, body(): targets = lax.all_gather(packed, 'tgt', axis=1, tiled=True)  15.2 us
    psum x1, blocking collectives, body(): own_sum = lax.psum(own_share, 'src')  11.8 us
    unnamed x1, blocking collectives  9.85 us
    unnamed x18, local copies, waits for them, and re-layouts  5.27 us

commit v1 on v0

v1 whole, which is shorter than its diff:
```python
import functools

import jax
import jax.numpy as jnp
from jax import lax
from jax.experimental import pallas as pl
from jax.experimental.pallas import tpu as pltpu
from jax.sharding import PartitionSpec as P

CLUSTERS = 64
EPSILON = 1.0
MASS_FACTOR = 10.0 / 11.0
BARRED = -(2.0**100)
TERMS = 8
SMALL, LARGE = 4 << 20, 32 << 20

F32, BF16 = jnp.float32, jnp.bfloat16


def in_three(value):
    high = value.astype(BF16).astype(F32)
    rest = value - high
    middle = rest.astype(BF16).astype(F32)
    return high, middle, rest - middle


def square_norms(points):
    widened = points.astype(F32)
    return jnp.sum(widened * widened, axis=0, keepdims=True)


def pack_kernel(
    src_hbm, tgt_hbm, src_mass_hbm, tgt_mass_hbm, potential_hbm, src_label_hbm, tgt_label_hbm,
    packed_ref,
    src_ref, tgt_ref, src_mass_ref, tgt_mass_ref, potential_ref, src_label_ref, tgt_label_ref, sems,
):
    pairs = (
        (tgt_hbm, tgt_ref),
        (src_hbm, src_ref),
        (src_mass_hbm, src_mass_ref),
        (tgt_mass_hbm, tgt_mass_ref),
        (potential_hbm, potential_ref),
        (src_label_hbm, src_label_ref),
        (tgt_label_hbm, tgt_label_ref),
    )
    copies = [pltpu.make_async_copy(a, b, sems.at[n]) for n, (a, b) in enumerate(pairs)]
    for copy in copies:
        copy.start()
    for copy in copies:
        copy.wait()
    dim, rows = src_ref.shape
    columns = tgt_ref.shape[1]
    fold = columns // rows
    slab = dim // fold
    targets = tgt_ref[...]
    sources = src_ref[...]
    packed_ref[0:dim, :] = targets
    for part in range(fold):
        packed_ref[dim : dim + slab, part * rows : (part + 1) * rows] = sources[
            part * slab : (part + 1) * slab
        ]
    tgt_mass = tgt_mass_ref[...].astype(F32).reshape(1, columns)
    potential = potential_ref[...].astype(F32).reshape(1, columns)
    row_bias = (potential - square_norms(targets)) / EPSILON + tgt_mass
    tgt_label = tgt_label_ref[...].astype(F32).reshape(1, columns)
    src_norms = square_norms(sources)
    src_rest = src_mass_ref[...].reshape(1, rows) - src_norms / EPSILON
    src_label = src_label_ref[...].astype(F32).reshape(1, rows)
    lines = [*in_three(row_bias), tgt_label]
    narrow = [src_label, *in_three(src_norms), *in_three(src_rest)]
    narrow += [jnp.zeros((1, rows), F32)] * (-len(narrow) % fold)
    for start in range(0, len(narrow), fold):
        lines.append(jnp.concatenate(narrow[start : start + fold], axis=1))
    place = lax.broadcasted_iota(jnp.int32, (TERMS, columns), 0)
    terms = jnp.zeros((TERMS, columns), F32)
    for number, line in enumerate(lines):
        terms = jnp.where(place == number, line, terms)
    packed_ref[dim + slab : dim + slab + TERMS, :] = terms.astype(BF16)


def grid_kernel(pairs_ref, grid_ref):
    count = pairs_ref.shape[1]
    names = lax.broadcasted_iota(jnp.int32, (CLUSTERS, count), 0)
    src_side = (names == pairs_ref[0:1, :]).astype(F32).astype(BF16)
    tgt_side = (names == pairs_ref[1:2, :]).astype(F32).astype(BF16)
    grid = lax.dot_general(
        tgt_side, src_side, (((1,), (1,)), ((), ())), preferred_element_type=F32
    )
    grid_ref[...] = grid.astype(BF16)


def main_kernel(dim, rows, columns, spread, grid_ref, *refs):
    blocks, (new_src_hbm, share_ref, new_src_ref, sem) = refs[:-4], refs[-4:]
    leave = pltpu.make_async_copy(new_src_ref, new_src_hbm, sem)
    fold = columns // rows
    slab = dim // fold
    names_rows = lax.broadcasted_iota(jnp.int32, (CLUSTERS, rows), 0).astype(F32)
    names_columns = lax.broadcasted_iota(jnp.int32, (CLUSTERS, columns), 0).astype(F32)
    place = lax.broadcasted_iota(jnp.int32, (TERMS, 2 * 128), 0)
    half = lax.broadcasted_iota(jnp.int32, (TERMS, 2 * 128), 1) < 128
    picked = jnp.where(
        half, (place < 3).astype(F32), ((place >= 3) & (place < 6)).astype(F32)
    ).astype(BF16)
    left, right, biases, norms, rests = [], [], [], [], []
    for block in blocks:
        terms = block[dim + slab :, :].astype(F32)
        biases.append(terms[0:1] + terms[1:2] + terms[2:3])
        tgt_onehot = (names_columns == terms[3:4]).astype(F32).astype(BF16)
        right.append(jnp.concatenate([block[0:dim, :], tgt_onehot], axis=0))
        narrow = [
            terms[4 + n // fold : 5 + n // fold, (n % fold) * rows : (n % fold + 1) * rows]
            for n in range(7)
        ]
        src_onehot = (names_rows == narrow[0]).astype(F32).astype(BF16)
        kept = jnp.dot(grid_ref[...], src_onehot, preferred_element_type=F32)
        penalty = ((1.0 - kept) * BARRED).astype(BF16)
        sources = jnp.concatenate(
            [
                block[dim : dim + slab, part * rows : (part + 1) * rows].astype(F32)
                for part in range(fold)
            ],
            axis=0,
        )
        left.append(jnp.concatenate([(2.0 / EPSILON * sources).astype(BF16), penalty], axis=0))
        side_place = lax.broadcasted_iota(jnp.int32, (TERMS, rows), 0)
        side = jnp.zeros((TERMS, rows), F32)
        for n in range(6):
            side = jnp.where(side_place == n, narrow[n + 1], side)
        both = lax.dot_general(
            side.astype(BF16), picked, (((0,), (0,)), ((), ())), preferred_element_type=F32
        )
        norms.append(both[:, 0:1])
        rests.append(both[:, 128:129])
    own_norms = square_norms(blocks[0][0:dim, :])
    own_scores, col_biases = [], []
    for number in range(len(blocks)):
        scores = [
            lax.dot_general(
                left[number], side, (((0,), (0,)), ((), ())), preferred_element_type=F32
            )
            for side in right
        ]
        own_scores.append(scores[0])
        biased = [score + bias for score, bias in zip(scores, biases, strict=True)]
        highest = functools.reduce(jnp.maximum, [jnp.max(b, 1, keepdims=True) for b in biased])
        total = sum(jnp.sum(jnp.exp(b - highest), 1, keepdims=True) for b in biased)
        norm = norms[number]
        new_src = -MASS_FACTOR * EPSILON * (highest + jnp.log(total) - norm / EPSILON)
        col_biases.append(new_src / EPSILON + rests[number])
        if number == 0:
            wide = jnp.broadcast_to(new_src, (rows, 128))
            new_src_ref[...] = wide.T[0:1, :]
            leave.start()
    shifted = [score + bias for score, bias in zip(own_scores, col_biases, strict=True)]
    peak = functools.reduce(jnp.maximum, [jnp.max(s, 0, keepdims=True) for s in shifted])
    mass = sum(jnp.sum(jnp.exp(s - peak), 0, keepdims=True) for s in shifted)
    share = peak + jnp.log(mass) - own_norms / EPSILON
    share_ref[...] = jnp.broadcast_to(share[None], (spread, 1, columns))
    leave.wait()


def tail_kernel(shares_ref, new_tgt_ref):
    shares = shares_ref[...][:, 0, :]
    peak = jnp.max(shares, axis=0, keepdims=True)
    total = jnp.sum(jnp.exp(shares - peak), axis=0, keepdims=True)
    new_tgt_ref[...] = -MASS_FACTOR * EPSILON * (peak + jnp.log(total))


def vmem(count):
    return [pl.BlockSpec(memory_space=pltpu.VMEM)] * count


def partners(count):
    if count & (count - 1) == 0:
        return [[(i, i ^ k) for i in range(count)] for k in range(1, count)]
    return [[(i, (i + k) % count) for i in range(count)] for k in range(1, count)]


def solution(mesh):
    src_size, tgt_size = mesh.shape["src"], mesh.shape["tgt"]

    def body(
        src_points, tgt_points, src_log_mass, tgt_log_mass, tgt_potential, src_cluster, tgt_cluster,
        kept_pairs,
    ):
        dim, rows = src_points.shape
        columns = tgt_points.shape[1]
        height = dim + dim * rows // columns + TERMS
        arrays = (
            src_points, tgt_points, src_log_mass, tgt_log_mass, tgt_potential, src_cluster,
            tgt_cluster,
        )
        packed = pl.pallas_call(
            pack_kernel,
            out_shape=jax.ShapeDtypeStruct((height, columns), BF16),
            in_specs=[pl.BlockSpec(memory_space=pltpu.HBM)] * len(arrays),
            out_specs=vmem(1)[0],
            scratch_shapes=[pltpu.VMEM(a.shape, a.dtype) for a in arrays]
            + [pltpu.SemaphoreType.DMA((len(arrays),))],
            name="pack",
            compiler_params=pltpu.CompilerParams(vmem_limit_bytes=SMALL),
        )(*[pltpu.with_memory_space_constraint(a, pltpu.HBM) for a in arrays])
        others = [lax.ppermute(packed, "tgt", pairs) for pairs in partners(tgt_size)]
        grid = pl.pallas_call(
            grid_kernel,
            out_shape=jax.ShapeDtypeStruct((CLUSTERS, CLUSTERS), BF16),
            in_specs=vmem(1),
            out_specs=vmem(1)[0],
            name="grid",
            compiler_params=pltpu.CompilerParams(vmem_limit_bytes=SMALL),
        )(kept_pairs.T)
        new_src, share = pl.pallas_call(
            functools.partial(main_kernel, dim, rows, columns, src_size),
            out_shape=(
                jax.ShapeDtypeStruct((1, rows), F32),
                jax.ShapeDtypeStruct((src_size, 1, columns), F32),
            ),
            in_specs=vmem(1 + tgt_size),
            out_specs=(pl.BlockSpec(memory_space=pltpu.HBM), vmem(1)[0]),
            scratch_shapes=[pltpu.VMEM((1, rows), F32), pltpu.SemaphoreType.DMA],
            name="halves",
            compiler_params=pltpu.CompilerParams(vmem_limit_bytes=LARGE),
        )(grid, packed, *others)
        shares = lax.all_to_all(share, "src", split_axis=0, concat_axis=0, tiled=True)
        new_tgt = pl.pallas_call(
            tail_kernel,
            out_shape=jax.ShapeDtypeStruct((1, columns), F32),
            in_specs=vmem(1),
            out_specs=vmem(1)[0],
            name="tail",
            compiler_params=pltpu.CompilerParams(vmem_limit_bytes=SMALL),
        )(shares)
        return new_src.reshape(rows), new_tgt.reshape(columns)

    in_specs = (
        P(None, ("src", "tgt")),
        P(None, "tgt"),
        P(("src", "tgt")),
        P("tgt"),
        P("tgt"),
        P(("src", "tgt")),
        P("tgt"),
        P(),
    )
    out_specs = (P(("src", "tgt")), P("tgt"))
    return jax.shard_map(body, mesh=mesh, in_specs=in_specs, out_specs=out_specs, check_vma=False)
```

time: 93.2 us -> 22.2 us (0.24)
  blocking collectives: 77.7 us -> 8.23 us
  starting transfers between devices: 0 us -> 5.78 us
  local copies, waits for them, and re-layouts: 5.31 us -> 0.01 us
  other arithmetic: 4.79 us -> 0 us
  waiting for transfers between devices: 0 us -> 4.2 us
  Pallas kernels: 0 us -> 3.1 us
  matrix products: 2.63 us -> 0 us
  between operations: 2.03 us -> 0.67 us
    pmax x1 -> x0, blocking collectives: 40.9 us -> none  [body(): global_peak = lax.pmax(col_peak, ('src', 'tgt'))]
    all_gather x1 -> x0, blocking collectives: 15.2 us -> none  [body(): targets = lax.all_gather(packed, 'tgt', axis=1, tiled=True)]
    psum x1 -> x0, blocking collectives: 11.8 us -> none  [body(): own_sum = lax.psum(own_share, 'src')]
    unnamed x1 -> x0, blocking collectives: 9.85 us -> none
    all_to_all x0 -> x1, blocking collectives: none -> 8.23 us  [body(): lax.all_to_all(share, 'src', split_axis=0, concat_axis=0, tiled=True)]
    ppermute x0 -> x3, starting transfers between devices: none -> 5.78 us  [body(): lax.ppermute(packed, 'tgt', pairs)]
    unnamed x18 -> x2, local copies, waits for them, and re-layouts: 5.27 us -> 0.01 us
    ppermute x0 -> x3, waiting for transfers between devices: none -> 4.2 us  [body(): lax.ppermute(packed, 'tgt', pairs)]
  transfers between devices with their start and end apart: 0 -> 3, of which waited for: 0 -> 2; matrix products, arithmetic and copies ran while one was open for 0% -> 0% of each run, Pallas kernels for 0% -> 1%
where the time goes in v1:
time: 22.2 us; the launch traced here: 22 us
  blocking collectives  8.23 us (37%)
  starting transfers between devices  5.78 us (26%)
  waiting for transfers between devices  4.2 us (19%)
  Pallas kernels  3.1 us (14%)
  between operations  0.67 us (3%)
    all_to_all x1, blocking collectives, body(): lax.all_to_all(share, 'src', split_axis=0, concat_axis=0, tiled=True)  8.23 us
    ppermute x3, starting transfers between devices, body(): lax.ppermute(packed, 'tgt', pairs)  5.78 us
    ppermute x3, waiting for transfers between devices, body(): lax.ppermute(packed, 'tgt', pairs)  4.2 us
    pallas_call x1, Pallas kernels, body(): pl.pallas_call(functools.partial(main_kernel, dim, rows, columns, src_siz...  1.45 us
    pallas_call x1, Pallas kernels, body(): pl.pallas_call(pack_kernel, out_shape=jax.ShapeDtypeStruct((height, colum...  0.87 us
    pallas_call x1, Pallas kernels, body(): pl.pallas_call(tail_kernel, out_shape=jax.ShapeDtypeStruct((1, columns),...  0.6 us
  transfers between devices with their start and end apart: 3, of which 2 were waited for; matrix products, arithmetic and copies ran while one was open for 0% of the time, Pallas kernels for 1%

profile of v1, /device:TPU:0, one launch (start us, length us, event | category | flops | bytes accessed | tf_op | source)
XLA Modules:
  0.0 22.0 jit_solution(16265112110859270322)
XLA Ops:
  0.6 0.0 copy-start
  0.6 0.9 %pack.1.refs_0_ = bf16[104,256]{1,0:T(8,128)(2,1)S(1)} custom-call(bf16[64,128]{1,0:T(8,128)(2,1)} %src_hbm.1, bf16[64,256]{1,0:T(8,128)(2,1)} %tgt_hbm.1, f32[128]{0:T(128)} %src_mass_hbm.1, bf16[256]{0:T(256)(128)(2,1)} %tgt_mass_hbm.1, bf16[256]{0:T(256)(128)(2,1)} %potential_hbm.1, s32[128]{0:T(128)} %src_label_hbm.1, s32[256]{0:T(256)} %tgt_label_hbm.1), custom_call_target="tpu_custom_call" | custom-call | tf_op jit(solution)/shard_map/pack/pallas_call | solution.py:193
  1.5 5.1 %collective-permute-start.2 = (bf16[104,256]{1,0:T(8,128)(2,1)S(1)}, bf16[104,256]{1,0:T(8,128)(2,1)S(1)}, u32[]{:S(2)}, u32[]{:S(2)}) collective-permute-start(bf16[104,256]{1,0:T(8,128)(2,1)S(1)} %pack.1.refs_0_), channel_id=1, source_target_pairs={{0,3},{1,2},{2,1},{3,0},{4,7},{5,6},{6,5},{7,4},{8,11},{9,10},{10,... | collective-permute-start | bytes 159752 | tf_op jit(solution)/shard_map/ppermute | solution.py:203
  6.7 0.0 collective-permute-start.1
  6.7 0.6 %collective-permute-start = (bf16[104,256]{1,0:T(8,128)(2,1)S(1)}, bf16[104,256]{1,0:T(8,128)(2,1)S(1)}, u32[]{:S(2)}, u32[]{:S(2)}) collective-permute-start(bf16[104,256]{1,0:T(8,128)(2,1)S(1)} %pack.1.refs_0_), channel_id=1, source_target_pairs={{0,1},{1,0},{2,3},{3,2},{4,5},{5,4},{6,7},{7,6},{8,9},{9,8},{10,11... | collective-permute-start | bytes 159752 | tf_op jit(solution)/shard_map/ppermute | solution.py:203
  7.3 0.0 copy-done
  7.3 0.2 grid.1.grid_ref
  7.5 1.4 %collective-permute-done.2.refs_3_ = bf16[104,256]{1,0:T(8,128)(2,1)S(1)} collective-permute-done((bf16[104,256]{1,0:T(8,128)(2,1)S(1)}, bf16[104,256]{1,0:T(8,128)(2,1)S(1)}, u32[]{:S(2)}, u32[]{:S(2)}) %collective-permute-start.2) | collective-permute-done | bytes 53280 | tf_op jit(solution)/shard_map/ppermute | solution.py:203
  8.9 2.8 %collective-permute-done.1.refs_2_ = bf16[104,256]{1,0:T(8,128)(2,1)S(1)} collective-permute-done((bf16[104,256]{1,0:T(8,128)(2,1)S(1)}, bf16[104,256]{1,0:T(8,128)(2,1)S(1)}, u32[]{:S(2)}, u32[]{:S(2)}) %collective-permute-start.1) | collective-permute-done | bytes 53280 | tf_op jit(solution)/shard_map/ppermute | solution.py:203
  11.7 0.0 collective-permute-done.refs_1_
  11.7 1.5 %halves.1 = (f32[1,128]{1,0:T(1,128)}, f32[8,1,256]{2,1,0:T(1,128)S(1)}) custom-call(bf16[64,64]{1,0:T(8,128)(2,1)S(1)} %grid.1.grid_ref, bf16[104,256]{1,0:T(8,128)(2,1)S(1)} %pack.1.refs_0_, bf16[104,256]{1,0:T(8,128)(2,1)S(1)} %collective-permute-done.refs_1_, bf16[104,256]{1,0:T(8,128)(2,1)S(1)} %collective-permute-done.1.refs_2_, ...), custom_call_target="tpu_custom_call" | custom-call | tf_op jit(solution)/shard_map/halves/pallas_call | solution.py:212
  13.2 8.2 %all_to_all.5.shares_ref = f32[8,1,256]{2,1,0:T(1,128)S(1)} all-to-all(f32[8,1,256]{2,1,0:T(1,128)S(1)} %get-tuple-element.5), channel_id=1, replica_groups=mesh['src'=8,'tgt'=4] {'src'}, dimensions={0} | all-to-all | bytes 16384 | tf_op jit(solution)/shard_map/all_to_all | solution.py:224
  21.4 0.6 %tail.1 = f32[1,256]{1,0:T(1,128)} custom-call(f32[8,1,256]{2,1,0:T(1,128)S(1)} %all_to_all.5.shares_ref), custom_call_target="tpu_custom_call" | custom-call | tf_op jit(solution)/shard_map/tail/pallas_call | solution.py:225
Async XLA Ops:
  0.6 6.7 %copy-start = (s32[1024,2]{0,1:T(2,128)S(1)}, s32[1024,2]{0,1:T(2,128)}, u32[]{:S(2)}) copy-start(s32[1024,2]{0,1:T(2,128)} %param.15) | copy-start | bytes 24580
  1.5 7.4 %collective-permute-start.2 = (bf16[104,256]{1,0:T(8,128)(2,1)S(1)}, bf16[104,256]{1,0:T(8,128)(2,1)S(1)}, u32[]{:S(2)}, u32[]{:S(2)}) collective-permute-start(bf16[104,256]{1,0:T(8,128)(2,1)S(1)} %pack.1.refs_0_), channel_id=1, source_target_pairs={{0,3},{1,2},{2,1},{3,0},{4,7},{5,6},{6,5},{7,4},{8,11},{9,10},{10,... | collective-permute-start | bytes 159752 | tf_op jit(solution)/shard_map/ppermute | solution.py:203
  6.7 5.0 %collective-permute-start.1 = (bf16[104,256]{1,0:T(8,128)(2,1)S(1)}, bf16[104,256]{1,0:T(8,128)(2,1)S(1)}, u32[]{:S(2)}, u32[]{:S(2)}) collective-permute-start(bf16[104,256]{1,0:T(8,128)(2,1)S(1)} %pack.1.refs_0_), channel_id=1, source_target_pairs={{0,2},{1,3},{2,0},{3,1},{4,6},{5,7},{6,4},{7,5},{8,10},{9,11},{10,... | collective-permute-start | bytes 159752 | tf_op jit(solution)/shard_map/ppermute | solution.py:203
  6.7 5.0 %collective-permute-start = (bf16[104,256]{1,0:T(8,128)(2,1)S(1)}, bf16[104,256]{1,0:T(8,128)(2,1)S(1)}, u32[]{:S(2)}, u32[]{:S(2)}) collective-permute-start(bf16[104,256]{1,0:T(8,128)(2,1)S(1)} %pack.1.refs_0_), channel_id=1, source_target_pairs={{0,1},{1,0},{2,3},{3,2},{4,5},{5,4},{6,7},{7,6},{8,9},{9,8},{10,11... | collective-permute-start | bytes 159752 | tf_op jit(solution)/shard_map/ppermute | solution.py:203
